TPU v7x, 256 devices: a whole 4x4x8 slice. The times are simulated.
256 devices in a mesh: row: 8 (over x, core), rhs: 32 (over y, z).
Axes of the slice: x: 4, y: 4, z: 8, core: 2. Of those that a mesh axis runs over, the one named last changes fastest.
Arguments:
- local_rhs: bfloat16 [336, 128, 4096], P('row', None, 'rhs'), may hold values from -6 to 6
- top_rhs: bfloat16 [8, 128, 4096], P('row', None, 'rhs'), may hold values from -6 to 6
- diag_inv: bfloat16 [336, 128, 128], P('row', 'rhs'), as said below
- top_inv: bfloat16 [8, 128, 128], P('row', 'rhs'), as said below
- off_blocks: bfloat16 [336, 4, 128, 128], P('row', None, 'rhs'), may hold values from -0.125 to 0.125
- top_factor: bfloat16 [8, 8, 128, 128], P('row', None, 'rhs'), may hold values from -0.1875 to 0.1875
- targets: int32 [336, 4], P('row'), may hold values from 24 to 49, as said below
Outputs:
- local_solution: bfloat16 [336, 128, 4096], P('row', None, 'rhs')
- top_solution: bfloat16 [8, 128, 4096], P('row', None, 'rhs')
Inputs may be any that keep to these rules, and one draw needn't show every extreme that they name: `diag_inv`: each block is lower triangular. `top_inv`: each block is lower triangular. `targets`: row r * 42 + k holds 4 distinct codes; a code c < 42 names local supernode r * 42 + c, of a higher level than k; a code c >= 42 names top block c - 42.
All inputs are finite; a program needn't handle non-finite values.
Results may differ from a plain program's by a relative error of at most 0.023.
Values may be sent and summed in bfloat16 or wider, within the bound.
No kernel may reach another device: no remote copies, remote signals or barrier semaphores. Data moves between devices by JAX's collectives and lax.ppermute only.
A program may use at most 64 MiB of HBM per device.

v0:
```python
import jax
import jax.numpy as jnp
from jax import lax
from jax.sharding import PartitionSpec as P

LEAF = 24


def spread(shard, axis, root):
    mine = lax.axis_index(axis) == root
    return lax.psum(jnp.where(mine, shard, jnp.zeros_like(shard)), axis)


def local(local_rhs, top_rhs, diag_inv, top_inv, off_blocks, top_factor, targets):
    sub_count = local_rhs.shape[0]
    panel_width = local_rhs.shape[1]
    columns = local_rhs.shape[2]
    top_count = lax.axis_size("row")
    cand_count = sub_count + top_count
    acc_local = jnp.zeros((sub_count, panel_width, columns), jnp.float32)
    acc_top = jnp.zeros((top_count, panel_width, columns), jnp.float32)
    level_ranges = ((0, LEAF), (LEAF, LEAF + LEAF // 2), (LEAF + LEAF // 2, sub_count))
    solved = []
    for first_row, end_row in level_ranges:
        residual_rows = (
            local_rhs[first_row:end_row].astype(jnp.float32) - acc_local[first_row:end_row]
        ).astype(jnp.bfloat16)

        def apply_inverse(slice_part, offset, residual_rows=residual_rows):
            return jnp.einsum(
                "jxm,jme->jxe", slice_part, residual_rows, preferred_element_type=jnp.float32
            )

        level_partial = apply_inverse(
            lax.all_gather(diag_inv[first_row:end_row], "rhs", axis=1, tiled=True), jnp.int32(0)
        ).astype(jnp.bfloat16)
        solved.append(level_partial)
        target_codes = targets[first_row:end_row].reshape(-1)
        later_count = cand_count - end_row
        selector = (
            jnp.arange(later_count, dtype=jnp.int32)[:, None] == target_codes[None, :] - end_row
        ).astype(jnp.float32)

        def spread_updates(slice_part, offset, level_partial=level_partial, selector=selector):
            products = jnp.einsum(
                "yiko,yoq->yikq", slice_part, level_partial, preferred_element_type=jnp.float32
            )
            flattened = products.reshape(selector.shape[1], slice_part.shape[2], columns)
            return jnp.einsum("cn,nar->car", selector, flattened, precision=lax.Precision.HIGHEST)

        contrib = spread_updates(
            lax.all_gather(off_blocks[first_row:end_row], "rhs", axis=2, tiled=True), jnp.int32(0)
        )
        acc_local = acc_local.at[end_row:].add(contrib[: sub_count - end_row])
        acc_top = acc_top + contrib[sub_count - end_row :]
    inverse_rows = top_inv.reshape(1, 1, top_inv.shape[1], panel_width)
    top_full, inv_full = (
        lax.all_gather(top_factor, "rhs", axis=2, tiled=True),
        lax.all_gather(inverse_rows, "rhs", axis=2, tiled=True),
    )
    position = lax.axis_index("row")
    own_sum = lax.psum_scatter(
        acc_top.astype(jnp.bfloat16), "row", scatter_dimension=0, tiled=True
    ).astype(jnp.float32)
    base_value = top_rhs[0].astype(jnp.float32) - own_sum[0]

    def top_step(step_index, carry):
        carried, own_solution = carry
        residual_rows = (base_value - carried).astype(jnp.bfloat16)
        candidate = jnp.dot(
            inv_full[0, 0], residual_rows, preferred_element_type=jnp.float32
        ).astype(jnp.bfloat16)
        solution = spread(candidate, "row", step_index)
        own_solution = jnp.where(position == step_index, solution, own_solution)
        coupling_matrix = lax.dynamic_index_in_dim(top_full[0], step_index, 0, keepdims=False)
        update = jnp.dot(coupling_matrix, solution, preferred_element_type=jnp.float32)
        carried = carried + jnp.where(step_index < position, update, 0.0)
        return (carried, own_solution)

    initial_state = (
        jnp.zeros((panel_width, columns), jnp.float32),
        jnp.zeros((panel_width, columns), jnp.bfloat16),
    )
    own_separator = lax.fori_loop(0, top_count, top_step, initial_state)[1][None]
    return (jnp.concatenate(solved, axis=0), own_separator)


def solution(mesh):
    in_specs = (
        P("row", None, "rhs"),
        P("row", None, "rhs"),
        P("row", "rhs", None),
        P("row", "rhs", None),
        P("row", None, "rhs", None),
        P("row", None, "rhs", None),
        P("row", None),
    )
    out_specs = (P("row", None, "rhs"), P("row", None, "rhs"))
    return jax.shard_map(local, mesh=mesh, in_specs=in_specs, out_specs=out_specs, check_vma=False)
```

profile of v0, /device:TPU:16, one launch (start us, length us, event | category | flops | bytes accessed | tf_op | source)
XLA Modules:
  0.0 551.3 jit_solution(5138594552302585885)
XLA Ops:
  7.3 0.9 slice.103
  8.9 0.9 slice.109
  10.6 0.8 slice.99
  12.1 54.8 %all_gather.28 = bf16[6,128,128]{2,0,1:T(8,128)(2,1)} all-gather(bf16[6,4,128]{2,0,1:T(8,128)(2,1)S(1)} %copy.125), channel_id=1, replica_groups=mesh['row'=8,'rhs'=32] {'rhs'}, dimensions={1}, use_global_device_ids=true | all-gather | bytes 202752 | tf_op jit(solution)/shard_map/all_gather | solution.py:35
  66.9 48.5 %all_gather.26 = bf16[12,128,128]{2,0,1:T(8,128)(2,1)S(1)} all-gather(bf16[12,4,128]{2,0,1:T(8,128)(2,1)S(1)} %copy.122), channel_id=1, replica_groups=mesh['row'=8,'rhs'=32] {'rhs'}, dimensions={1}, use_global_device_ids=true | all-gather | bytes 405504 | tf_op jit(solution)/shard_map/all_gather | solution.py:35
  115.4 47.8 %all_gather.24 = bf16[24,128,128]{2,0,1:T(8,128)(2,1)S(1)} all-gather(bf16[24,4,128]{2,0,1:T(8,128)(2,1)S(1)} %copy.119), channel_id=1, replica_groups=mesh['row'=8,'rhs'=32] {'rhs'}, dimensions={1}, use_global_device_ids=true | all-gather | bytes 811008 | tf_op jit(solution)/shard_map/all_gather | solution.py:35
  163.2 53.6 %all_gather.30 = bf16[6,4,128,128]{3,1,0,2:T(4,128)(2,1)} all-gather(bf16[6,4,4,128]{3,1,0,2:T(4,128)(2,1)S(1)} %copy.126), channel_id=1, replica_groups=mesh['row'=8,'rhs'=32] {'rhs'}, dimensions={2}, use_global_device_ids=true | all-gather | bytes 811008 | tf_op jit(solution)/shard_map/all_gather | solution.py:52
  217.3 7.2 %fusion.10 = f32[24,128,4,128]{3,1,2,0:T(8,128)} fusion(bf16[24,4,128,128]{3,0,1,2:T(8,128)(2,1)} %all-gather.4.cloned.1.call-done, bf16[24,128,128]{2,1,0:T(8,128)(2,1)S(1)} %convolution_convert_fusion.1), kind=kOutput, calls=%fused_computation.14 | convolution fusion | flops 402653184 | bytes 10223616 | tf_op jit(solution)/shard_map/yiko,yoq->yikq/dot_general | solution.py:45
  224.5 6.7 %copy.82 = f32[96,128,128]{2,0,1:T(8,128)} copy(f32[96,128,128]{1,2,0:T(8,128)} %bitcast.61) | data formatting | bytes 12582912 | tf_op jit(solution)/shard_map/reshape | solution.py:48
  231.2 4.5 fusion.30
  235.8 1.4 copy-done
  237.8 3.8 fusion.12
  241.6 2.6 copy.92
  244.2 1.2 fusion.34
  245.4 1.9 fusion.22
  247.5 1.6 fusion.17
  249.1 2.0 copy.102
  251.2 2.0 fusion.14
  253.2 0.8 copy.103
  254.0 46.4 %all_gather.29 = bf16[1,8,128,128]{3,1,0,2:T(8,128)(2,1)S(1)} all-gather(bf16[1,8,4,128]{3,1,0,2:T(8,128)(2,1)S(1)} %copy.97), channel_id=1, replica_groups=mesh['row'=8,'rhs'=32] {'rhs'}, dimensions={2}, use_global_device_ids=true | all-gather | bytes 270336 | tf_op jit(solution)/shard_map/all_gather | solution.py:58
  300.5 48.1 %all-gather = bf16[1,128,128]{2,0,1:T(2,128)(2,1)S(1)} all-gather(bf16[1,4,128]{2,0,1:T(2,128)(2,1)S(1)} %copy.104), channel_id=2, replica_groups=mesh['row'=8,'rhs'=32] {'rhs'}, dimensions={1}, use_global_device_ids=true | all-gather | bytes 33792 | tf_op jit(solution)/shard_map/all_gather | solution.py:59
  348.7 2.3 pad_maximum_fusion
  351.0 0.8 subtract_bitcast_fusion
  351.8 192.2 %while.18 = (s32[]{:T(128)}, f32[128,128]{1,0:T(8,128)S(1)}, bf16[128,128]{0,1:T(8,128)(2,1)S(1)}, s32[]{:T(128)}, bf16[1,8,128,128]{3,2,1,0:T(8,128)(2,1)S(1)},...) while((s32[]{:T(128)}, f32[128,128]{1,0:T(8,128)S(1)}, ...), condition=%wide.region_3.4_spmd.clone, body=%wide.region_1.3_spmd.clone.sunk | while | flops 8568841 | bytes 557243 | solution.py:84
  352.0 23.6 %psum.13 = bf16[128,128]{0,1:T(8,128)(2,1)S(1)} all-reduce(bf16[128,128]{0,1:T(8,128)(2,1)S(1)} %fusion.52), channel_id=1, replica_groups=mesh['row'=8,'rhs'=32] {'row'}, use_global_device_ids=true, to_apply=%region_2.2 | all-reduce | flops 16384 | bytes 65536 | tf_op jit(solution)/shard_map/while/body/eval_jaxpr/psum | solution.py:11
  376.1 23.6 %psum.13 = bf16[128,128]{0,1:T(8,128)(2,1)S(1)} all-reduce(bf16[128,128]{0,1:T(8,128)(2,1)S(1)} %fusion.52), channel_id=1, replica_groups=mesh['row'=8,'rhs'=32] {'row'}, use_global_device_ids=true, to_apply=%region_2.2 | all-reduce | flops 16384 | bytes 65536 | tf_op jit(solution)/shard_map/while/body/eval_jaxpr/psum | solution.py:11
  400.1 23.6 %psum.13 = bf16[128,128]{0,1:T(8,128)(2,1)S(1)} all-reduce(bf16[128,128]{0,1:T(8,128)(2,1)S(1)} %fusion.52), channel_id=1, replica_groups=mesh['row'=8,'rhs'=32] {'row'}, use_global_device_ids=true, to_apply=%region_2.2 | all-reduce | flops 16384 | bytes 65536 | tf_op jit(solution)/shard_map/while/body/eval_jaxpr/psum | solution.py:11
  424.1 23.6 %psum.13 = bf16[128,128]{0,1:T(8,128)(2,1)S(1)} all-reduce(bf16[128,128]{0,1:T(8,128)(2,1)S(1)} %fusion.52), channel_id=1, replica_groups=mesh['row'=8,'rhs'=32] {'row'}, use_global_device_ids=true, to_apply=%region_2.2 | all-reduce | flops 16384 | bytes 65536 | tf_op jit(solution)/shard_map/while/body/eval_jaxpr/psum | solution.py:11
  448.1 23.6 %psum.13 = bf16[128,128]{0,1:T(8,128)(2,1)S(1)} all-reduce(bf16[128,128]{0,1:T(8,128)(2,1)S(1)} %fusion.52), channel_id=1, replica_groups=mesh['row'=8,'rhs'=32] {'row'}, use_global_device_ids=true, to_apply=%region_2.2 | all-reduce | flops 16384 | bytes 65536 | tf_op jit(solution)/shard_map/while/body/eval_jaxpr/psum | solution.py:11
  472.1 23.6 %psum.13 = bf16[128,128]{0,1:T(8,128)(2,1)S(1)} all-reduce(bf16[128,128]{0,1:T(8,128)(2,1)S(1)} %fusion.52), channel_id=1, replica_groups=mesh['row'=8,'rhs'=32] {'row'}, use_global_device_ids=true, to_apply=%region_2.2 | all-reduce | flops 16384 | bytes 65536 | tf_op jit(solution)/shard_map/while/body/eval_jaxpr/psum | solution.py:11
  496.2 23.6 %psum.13 = bf16[128,128]{0,1:T(8,128)(2,1)S(1)} all-reduce(bf16[128,128]{0,1:T(8,128)(2,1)S(1)} %fusion.52), channel_id=1, replica_groups=mesh['row'=8,'rhs'=32] {'row'}, use_global_device_ids=true, to_apply=%region_2.2 | all-reduce | flops 16384 | bytes 65536 | tf_op jit(solution)/shard_map/while/body/eval_jaxpr/psum | solution.py:11
  520.2 23.6 %psum.13 = bf16[128,128]{0,1:T(8,128)(2,1)S(1)} all-reduce(bf16[128,128]{0,1:T(8,128)(2,1)S(1)} %fusion.52), channel_id=1, replica_groups=mesh['row'=8,'rhs'=32] {'row'}, use_global_device_ids=true, to_apply=%region_2.2 | all-reduce | flops 16384 | bytes 65536 | tf_op jit(solution)/shard_map/while/body/eval_jaxpr/psum | solution.py:11
  (96 shorter events, 7.2 us)
Async XLA Ops:
  7.2 4.7 slice-start.2
  7.2 4.4 slice-start.3
  7.2 4.6 slice-start.4
  7.2 4.1 copy-start.11
  7.2 210.0 %all-gather.4.cloned.1.call-start = ((), (), s32[]{:S(2)}) async-start(), calls=%async_computation.1 | async-start | bytes 3244032 | tf_op jit(solution)/shard_map/all_gather | solution.py:52
  8.9 208.0 %copy-start.8 = (bf16[42,128,128]{2,1,0:T(8,128)(2,1)S(1)}, bf16[42,128,128]{2,1,0:T(8,128)(2,1)}, u32[]{:S(2)}) copy-start(bf16[42,128,128]{2,1,0:T(8,128)(2,1)} %param.13) | copy-start | bytes 4128772
  8.9 228.9 %all-gather.6.cloned.1.call-start = ((), (), s32[]{:S(2)}) async-start(), calls=%async_computation.2 | async-start | bytes 1622016 | tf_op jit(solution)/shard_map/all_gather | solution.py:52
  10.5 340.5 %reduce-scatter.2.cloned.1.call-start = ((), (), s32[]{:S(2)}) async-start(), calls=%async_computation.3 | async-start | bytes 294912 | tf_op jit(solution)/shard_map/reduce_scatter | solution.py:62
  217.2 7.3 %copy-start.1 = (bf16[24,128,128]{2,1,0:T(8,128)(2,1)}, bf16[24,128,128]{2,1,0:T(8,128)(2,1)S(1)}, u32[]{:S(2)}) copy-start(bf16[24,128,128]{2,1,0:T(8,128)(2,1)S(1)} %convolution_convert_fusion.1) | copy-start | bytes 2359300
  231.2 5.9 %slice-start = ((bf16[42,128,128]{2,1,0:T(8,128)(2,1)}), bf16[12,128,128]{2,1,0:T(8,128)(2,1)S(1)}, s32[]{:S(2)}) async-start(bf16[42,128,128]{2,1,0:T(8,128)(2,1)} %param.13), calls=%async_computation.4 | async-start | bytes 786432 | tf_op jit(solution)/shard_map/slice | solution.py:26
  235.7 1.4 copy-start
  237.7 3.8 copy-start.5
  244.1 1.2 slice-start.1
  244.2 3.1 copy-start.9
  245.4 3.7 copy-start.3
  245.4 2.1 copy-start.6
  247.5 1.6 copy-start.7
  249.1 2.1 copy-start.4
  251.2 2.9 copy-start.12
  251.2 49.3 %copy-start.13 = (bf16[1,4,128]{2,1,0:T(4,128)(2,1)S(1)}, bf16[1,4,128]{2,1,0:T(4,128)(2,1)}, u32[]{:S(2)}) copy-start(bf16[1,4,128]{2,1,0:T(4,128)(2,1)} %param.16) | copy-start | bytes 3076
  251.2 97.5 %copy-start.2 = (bf16[24,128,128]{2,1,0:T(8,128)(2,1)S(1)}, bf16[24,128,128]{2,1,0:T(8,128)(2,1)}, u32[]{:S(2)}) copy-start(bf16[24,128,128]{2,1,0:T(8,128)(2,1)} %copy-done.1) | copy-start | bytes 2359300
  254.0 97.1 %copy-start.10 = (bf16[1,128,128]{2,1,0:T(8,128)(2,1)S(1)}, bf16[1,128,128]{2,1,0:T(8,128)(2,1)}, u32[]{:S(2)}) copy-start(bf16[1,128,128]{2,1,0:T(8,128)(2,1)} %param.14) | copy-start | bytes 98308
Sparse Core Ops, SparseCore 0:
  11.2 81.3 all-gather.3
  95.1 74.5 all-gather.5
  254.1 30.7 reduce-scatter.1
where the time goes:
time: 552 us; the launch traced here: 551 us
  blocking collectives  488 us (88%)
  matrix products  23.9 us (4%)
  local copies, waits for them, and re-layouts  18.8 us (3%)
  between operations  14.2 us (3%)
  other arithmetic  5.59 us (1%)
    psum x8, blocking collectives, spread(): return lax.psum(jnp.where(mine, shard, jnp.zeros_like(shard)), axis)  189 us
    all_gather x3, blocking collectives, local(): lax.all_gather(diag_inv[first_row:end_row], 'rhs', axis=1, tiled=True)  151 us
    all_gather x1, blocking collectives, local(): lax.all_gather(off_blocks[first_row:end_row], 'rhs', axis=2, tiled=True)  53.6 us
    all_gather x1, blocking collectives, local(): lax.all_gather(inverse_rows, 'rhs', axis=2, tiled=True)  48.1 us
    all_gather x1, blocking collectives, local(): lax.all_gather(top_factor, 'rhs', axis=2, tiled=True)  46.4 us
    dot_general x3, matrix products, spread_updates(): jnp.einsum('yiko,yoq->yikq', slice_part, level_partial, preferred_element...  12.6 us
    reshape x3, local copies, waits for them, and re-layouts, spread_updates(): products.reshape(selector.shape[1], slice_part.shape[2], columns)  11.4 us
  transfers between devices with their start and end apart: 3, of which 0 were waited for; matrix products, arithmetic and copies ran while one was open for 5% of the time, Pallas kernels for 0%

commit v1 on v0

--- a/solution.py
+++ b/solution.py
@@ -8,7 +8,7 @@
 
 def spread(shard, axis, root):
     mine = lax.axis_index(axis) == root
-    return lax.psum(jnp.where(mine, shard, jnp.zeros_like(shard)), axis)
+    return jnp.sum(lax.all_gather(jnp.where(mine, shard, jnp.zeros_like(shard)), axis), axis=0)
 
 
 def local(local_rhs, top_rhs, diag_inv, top_inv, off_blocks, top_factor, targets):

time: 552 us -> 461 us (0.84)
  blocking collectives: 488 us -> 392 us
    psum x8 -> x0, blocking collectives: 189 us -> none  [spread(): return lax.psum(jnp.where(mine, shard, jnp.zeros_like(shard)), axis)]
    all_gather x0 -> x8, blocking collectives: none -> 93.1 us  [spread(): lax.all_gather(jnp.where(mine, shard, jnp.zeros_like(shard)), axis)]
where the time goes in v1:
time: 461 us; the launch traced here: 458 us
  blocking collectives  392 us (85%)
  matrix products  23.9 us (5%)
  local copies, waits for them, and re-layouts  19.2 us (4%)
  between operations  14.2 us (3%)
  other arithmetic  7.16 us (2%)
    all_gather x3, blocking collectives, local(): lax.all_gather(diag_inv[first_row:end_row], 'rhs', axis=1, tiled=True)  151 us
    all_gather x8, blocking collectives, spread(): lax.all_gather(jnp.where(mine, shard, jnp.zeros_like(shard)), axis)  93.1 us
    all_gather x1, blocking collectives, local(): lax.all_gather(off_blocks[first_row:end_row], 'rhs', axis=2, tiled=True)  53.6 us
    all_gather x1, blocking collectives, local(): lax.all_gather(inverse_rows, 'rhs', axis=2, tiled=True)  48.1 us
    all_gather x1, blocking collectives, local(): lax.all_gather(top_factor, 'rhs', axis=2, tiled=True)  46.4 us
    dot_general x3, matrix products, spread_updates(): jnp.einsum('yiko,yoq->yikq', slice_part, level_partial, preferred_element...  12.6 us
    reshape x3, local copies, waits for them, and re-layouts, spread_updates(): products.reshape(selector.shape[1], slice_part.shape[2], columns)  11.4 us
  transfers between devices with their start and end apart: 3, of which 0 were waited for; matrix products, arithmetic and copies ran while one was open for 5% of the time, Pallas kernels for 0%

profile of v1, /device:TPU:16, one launch (start us, length us, event | category | flops | bytes accessed | tf_op | source)
XLA Modules:
  0.0 457.5 jit_solution(2576512213557467880)
XLA Ops:
  7.3 0.9 slice.103
  8.9 0.9 slice.109
  10.6 0.8 slice.99
  12.1 54.8 %all_gather.48 = bf16[6,128,128]{2,0,1:T(8,128)(2,1)} all-gather(bf16[6,4,128]{2,0,1:T(8,128)(2,1)S(1)} %copy.123), channel_id=1, replica_groups=mesh['row'=8,'rhs'=32] {'rhs'}, dimensions={1}, use_global_device_ids=true | all-gather | bytes 202752 | tf_op jit(solution)/shard_map/all_gather | solution.py:35
  66.9 48.5 %all_gather.46 = bf16[12,128,128]{2,0,1:T(8,128)(2,1)S(1)} all-gather(bf16[12,4,128]{2,0,1:T(8,128)(2,1)S(1)} %copy.120), channel_id=1, replica_groups=mesh['row'=8,'rhs'=32] {'rhs'}, dimensions={1}, use_global_device_ids=true | all-gather | bytes 405504 | tf_op jit(solution)/shard_map/all_gather | solution.py:35
  115.4 47.8 %all_gather.44 = bf16[24,128,128]{2,0,1:T(8,128)(2,1)S(1)} all-gather(bf16[24,4,128]{2,0,1:T(8,128)(2,1)S(1)} %copy.117), channel_id=1, replica_groups=mesh['row'=8,'rhs'=32] {'rhs'}, dimensions={1}, use_global_device_ids=true | all-gather | bytes 811008 | tf_op jit(solution)/shard_map/all_gather | solution.py:35
  163.2 53.6 %all_gather.50 = bf16[6,4,128,128]{3,1,0,2:T(4,128)(2,1)} all-gather(bf16[6,4,4,128]{3,1,0,2:T(4,128)(2,1)S(1)} %copy.124), channel_id=1, replica_groups=mesh['row'=8,'rhs'=32] {'rhs'}, dimensions={2}, use_global_device_ids=true | all-gather | bytes 811008 | tf_op jit(solution)/shard_map/all_gather | solution.py:52
  217.3 7.2 %fusion.10 = f32[24,128,4,128]{3,1,2,0:T(8,128)} fusion(bf16[24,4,128,128]{3,0,1,2:T(8,128)(2,1)} %all-gather.8.cloned.1.call-done, bf16[24,128,128]{2,1,0:T(8,128)(2,1)S(1)} %convolution_convert_fusion.1), kind=kOutput, calls=%fused_computation.15 | convolution fusion | flops 402653184 | bytes 10223616 | tf_op jit(solution)/shard_map/yiko,yoq->yikq/dot_general | solution.py:45
  224.5 6.7 %copy.80 = f32[96,128,128]{2,0,1:T(8,128)} copy(f32[96,128,128]{1,2,0:T(8,128)} %bitcast.71) | data formatting | bytes 12582912 | tf_op jit(solution)/shard_map/reshape | solution.py:48
  231.2 4.5 fusion.30
  235.8 1.4 copy-done
  237.8 3.8 fusion.12
  241.6 2.6 copy.90
  244.2 1.2 fusion.34
  245.4 1.9 fusion.22
  247.5 1.6 fusion.17
  249.1 2.0 copy.100
  251.2 2.0 fusion.14
  253.2 0.8 copy.101
  254.0 46.4 %all_gather.49 = bf16[1,8,128,128]{3,1,0,2:T(8,128)(2,1)S(1)} all-gather(bf16[1,8,4,128]{3,1,0,2:T(8,128)(2,1)S(1)} %copy.95), channel_id=1, replica_groups=mesh['row'=8,'rhs'=32] {'rhs'}, dimensions={2}, use_global_device_ids=true | all-gather | bytes 270336 | tf_op jit(solution)/shard_map/all_gather | solution.py:58
  300.5 48.1 %all-gather.1 = bf16[1,128,128]{2,0,1:T(2,128)(2,1)S(1)} all-gather(bf16[1,4,128]{2,0,1:T(2,128)(2,1)S(1)} %copy.102), channel_id=3, replica_groups=mesh['row'=8,'rhs'=32] {'rhs'}, dimensions={1}, use_global_device_ids=true | all-gather | bytes 33792 | tf_op jit(solution)/shard_map/all_gather | solution.py:59
  348.7 2.3 pad_maximum_fusion
  351.0 0.8 subtract_bitcast_fusion
  351.8 98.5 %while.20 = (s32[]{:T(128)}, f32[128,128]{1,0:T(8,128)S(1)}, bf16[128,128]{0,1:T(8,128)(2,1)S(1)}, s32[]{:T(128)}, bf16[1,8,128,128]{3,2,1,0:T(8,128)(2,1)S(1)},...) while((s32[]{:T(128)}, f32[128,128]{1,0:T(8,128)S(1)}, ...), condition=%wide.region_3.4_spmd.clone, body=%wide.region_1.3_spmd.clone.sunk | while | flops 8667145 | bytes 1605819 | solution.py:84
  352.0 12.0 %all-gather.4 = bf16[1024,128]{0,1:T(8,128)(2,1)S(1)} all-gather(bf16[128,128]{0,1:T(8,128)(2,1)S(1)} %fusion.52), channel_id=2, replica_groups=mesh['row'=8,'rhs'=32] {'row'}, dimensions={0}, use_global_device_ids=true | all-gather | bytes 294912 | tf_op jit(solution)/shard_map/while/body/eval_jaxpr/all_gather | solution.py:11
  364.7 11.5 %all-gather.4 = bf16[1024,128]{0,1:T(8,128)(2,1)S(1)} all-gather(bf16[128,128]{0,1:T(8,128)(2,1)S(1)} %fusion.52), channel_id=2, replica_groups=mesh['row'=8,'rhs'=32] {'row'}, dimensions={0}, use_global_device_ids=true | all-gather | bytes 294912 | tf_op jit(solution)/shard_map/while/body/eval_jaxpr/all_gather | solution.py:11
  376.9 11.7 %all-gather.4 = bf16[1024,128]{0,1:T(8,128)(2,1)S(1)} all-gather(bf16[128,128]{0,1:T(8,128)(2,1)S(1)} %fusion.52), channel_id=2, replica_groups=mesh['row'=8,'rhs'=32] {'row'}, dimensions={0}, use_global_device_ids=true | all-gather | bytes 294912 | tf_op jit(solution)/shard_map/while/body/eval_jaxpr/all_gather | solution.py:11
  389.3 11.5 %all-gather.4 = bf16[1024,128]{0,1:T(8,128)(2,1)S(1)} all-gather(bf16[128,128]{0,1:T(8,128)(2,1)S(1)} %fusion.52), channel_id=2, replica_groups=mesh['row'=8,'rhs'=32] {'row'}, dimensions={0}, use_global_device_ids=true | all-gather | bytes 294912 | tf_op jit(solution)/shard_map/while/body/eval_jaxpr/all_gather | solution.py:11
  401.4 11.7 %all-gather.4 = bf16[1024,128]{0,1:T(8,128)(2,1)S(1)} all-gather(bf16[128,128]{0,1:T(8,128)(2,1)S(1)} %fusion.52), channel_id=2, replica_groups=mesh['row'=8,'rhs'=32] {'row'}, dimensions={0}, use_global_device_ids=true | all-gather | bytes 294912 | tf_op jit(solution)/shard_map/while/body/eval_jaxpr/all_gather | solution.py:11
  413.8 11.5 %all-gather.4 = bf16[1024,128]{0,1:T(8,128)(2,1)S(1)} all-gather(bf16[128,128]{0,1:T(8,128)(2,1)S(1)} %fusion.52), channel_id=2, replica_groups=mesh['row'=8,'rhs'=32] {'row'}, dimensions={0}, use_global_device_ids=true | all-gather | bytes 294912 | tf_op jit(solution)/shard_map/while/body/eval_jaxpr/all_gather | solution.py:11
  426.0 11.7 %all-gather.4 = bf16[1024,128]{0,1:T(8,128)(2,1)S(1)} all-gather(bf16[128,128]{0,1:T(8,128)(2,1)S(1)} %fusion.52), channel_id=2, replica_groups=mesh['row'=8,'rhs'=32] {'row'}, dimensions={0}, use_global_device_ids=true | all-gather | bytes 294912 | tf_op jit(solution)/shard_map/while/body/eval_jaxpr/all_gather | solution.py:11
  438.3 11.5 %all-gather.4 = bf16[1024,128]{0,1:T(8,128)(2,1)S(1)} all-gather(bf16[128,128]{0,1:T(8,128)(2,1)S(1)} %fusion.52), channel_id=2, replica_groups=mesh['row'=8,'rhs'=32] {'row'}, dimensions={0}, use_global_device_ids=true | all-gather | bytes 294912 | tf_op jit(solution)/shard_map/while/body/eval_jaxpr/all_gather | solution.py:11
  (112 shorter events, 9.1 us)
Async XLA Ops:
  7.2 4.7 %slice-start.2 = ((bf16[42,4,4,128]{3,2,1,0:T(4,128)(2,1)}), bf16[6,4,4,128]{3,2,1,0:T(4,128)(2,1)S(1)}, s32[]{:S(2)}) async-start(bf16[42,4,4,128]{3,2,1,0:T(4,128)(2,1)} %param.17), calls=%async_computation.6 | async-start | bytes 49152 | tf_op jit(solution)/shard_map/slice | solution.py:52
  7.2 4.4 slice-start.3
  7.2 4.6 %slice-start.4 = ((bf16[42,4,128]{2,1,0:T(4,128)(2,1)}), bf16[6,4,128]{2,1,0:T(4,128)(2,1)S(1)}, s32[]{:S(2)}) async-start(bf16[42,4,128]{2,1,0:T(4,128)(2,1)} %param.15), calls=%async_computation.8 | async-start | bytes 12288 | tf_op jit(solution)/shard_map/slice | solution.py:35
  7.2 4.1 copy-start.11
  7.2 210.0 %all-gather.8.cloned.1.call-start = ((), (), s32[]{:S(2)}) async-start(), calls=%async_computation.1 | async-start | bytes 3244032 | tf_op jit(solution)/shard_map/all_gather | solution.py:52
  8.9 208.0 %copy-start.8 = (bf16[42,128,128]{2,1,0:T(8,128)(2,1)S(1)}, bf16[42,128,128]{2,1,0:T(8,128)(2,1)}, u32[]{:S(2)}) copy-start(bf16[42,128,128]{2,1,0:T(8,128)(2,1)} %param.13) | copy-start | bytes 4128772
  8.9 228.9 %all-gather.10.cloned.1.call-start = ((), (), s32[]{:S(2)}) async-start(), calls=%async_computation.2 | async-start | bytes 1622016 | tf_op jit(solution)/shard_map/all_gather | solution.py:52
  10.5 340.5 %reduce-scatter.2.cloned.1.call-start = ((), (), s32[]{:S(2)}) async-start(), calls=%async_computation.3 | async-start | bytes 294912 | tf_op jit(solution)/shard_map/reduce_scatter | solution.py:62
  217.2 7.3 %copy-start.1 = (bf16[24,128,128]{2,1,0:T(8,128)(2,1)}, bf16[24,128,128]{2,1,0:T(8,128)(2,1)S(1)}, u32[]{:S(2)}) copy-start(bf16[24,128,128]{2,1,0:T(8,128)(2,1)S(1)} %convolution_convert_fusion.1) | copy-start | bytes 2359300
  231.2 5.9 %slice-start = ((bf16[42,128,128]{2,1,0:T(8,128)(2,1)}), bf16[12,128,128]{2,1,0:T(8,128)(2,1)S(1)}, s32[]{:S(2)}) async-start(bf16[42,128,128]{2,1,0:T(8,128)(2,1)} %param.13), calls=%async_computation.4 | async-start | bytes 786432 | tf_op jit(solution)/shard_map/slice | solution.py:26
  235.7 1.4 copy-start
  237.7 3.8 copy-start.5
  244.1 1.2 slice-start.1
  244.2 3.1 copy-start.9
  245.4 3.7 copy-start.3
  245.4 2.1 copy-start.6
  247.5 1.6 copy-start.7
  249.1 2.1 copy-start.4
  251.2 2.9 copy-start.12
  251.2 49.3 %copy-start.13 = (bf16[1,4,128]{2,1,0:T(4,128)(2,1)S(1)}, bf16[1,4,128]{2,1,0:T(4,128)(2,1)}, u32[]{:S(2)}) copy-start(bf16[1,4,128]{2,1,0:T(4,128)(2,1)} %param.16) | copy-start | bytes 3076
  251.2 97.5 %copy-start.2 = (bf16[24,128,128]{2,1,0:T(8,128)(2,1)S(1)}, bf16[24,128,128]{2,1,0:T(8,128)(2,1)}, u32[]{:S(2)}) copy-start(bf16[24,128,128]{2,1,0:T(8,128)(2,1)} %copy-done.1) | copy-start | bytes 2359300
  254.0 97.1 %copy-start.10 = (bf16[1,128,128]{2,1,0:T(8,128)(2,1)S(1)}, bf16[1,128,128]{2,1,0:T(8,128)(2,1)}, u32[]{:S(2)}) copy-start(bf16[1,128,128]{2,1,0:T(8,128)(2,1)} %param.14) | copy-start | bytes 98308
Sparse Core Ops, SparseCore 0:
  11.2 81.3 all-gather.7
  95.1 74.5 all-gather.9
  254.1 30.7 reduce-scatter.1
